TPU v7x, 256 devices: a whole 4x4x8 slice. The times are simulated.
256 devices in a mesh: probe: 64 (over z, x_lo, y), slab: 4 (over x_hi, core).
Axes of the slice: x: 4 (x_hi: 2, x_lo: 2; x = x_hi * 2 + x_lo), y: 4, z: 8, core: 2. Of those that a mesh axis runs over, the one named last changes fastest.
Arguments:
- smatrix: bfloat16 [2, 512, 128, 128], P(None, 'probe', 'slab'), may hold values from -6 to 6
- amplitude: float32 [2, 512], replicated, may hold values from -0.25 to 0.25
- beam_index: int32 [512, 2], replicated, may hold values from -32 to 31
- positions: int32 [8192, 2], P('probe'), may hold values from -8 to 8
Outputs:
- patterns: float32 [8192, 128, 128], P('probe', 'slab')
Inputs may be any that keep to these rules, and one draw needn't show every extreme that they name: `positions`: column 0 is the row offset that places a probe's crop in the band, column 1 the column offset. `beam_index`: column 0 along rows, column 1 along columns.
All inputs are finite; a program needn't handle non-finite values.
Results may differ from a plain program's by a relative error of at most 0.0029.
Values may be sent and summed in bfloat16 or wider, within the bound.
A program may use at most 128 MiB of HBM per device.

v0:
```python
import math

import jax
import jax.numpy as jnp
from jax import lax
from jax.sharding import PartitionSpec as P

HALO = 8


def padded_2(x, sides, width):
    for axis, dim in sides:
        count, length = (lax.axis_size(axis), x.shape[dim])
        up = [(i, (i + 1) % count) for i in range(count - 1)]
        down = [(j, i) for i, j in up]
        last = lax.slice_in_dim(x, length - width, length, axis=dim)
        leading = lax.slice_in_dim(x, 0, width, axis=dim)
        before = lax.ppermute(last, axis, up)
        after = lax.ppermute(leading, axis, down)
        x = jnp.concatenate([before, x, after], axis=dim)
    return x


def beam_weights(amplitude, beam_index, place, rows_all, cols):
    row_phase = (
        jnp.mod(place[:, 0:1] * beam_index[None, :, 0], rows_all).astype(jnp.float32) / rows_all
    )
    col_phase = jnp.mod(place[:, 1:2] * beam_index[None, :, 1], cols).astype(jnp.float32) / cols
    angle = 2.0 * math.pi * (row_phase + col_phase)
    cosine = jnp.cos(angle)
    sine = jnp.sin(angle)
    real = amplitude[0][None, :] * cosine + amplitude[1][None, :] * sine
    imag = amplitude[1][None, :] * cosine - amplitude[0][None, :] * sine
    return (real.astype(jnp.bfloat16), imag.astype(jnp.bfloat16))


def dft_table(first, second, length):
    angle = (
        2.0
        * math.pi
        * (jnp.mod(first[:, None] * second[None, :], length).astype(jnp.float32) / length)
    )
    return (jnp.cos(angle), jnp.sin(angle))


def cut_rows(field, offset, count):
    return lax.dynamic_slice_in_dim(field, offset, count, 0)


def on_device(smatrix, amplitude, beam_index, positions):
    slab_rows = smatrix.shape[2]
    cols = smatrix.shape[3]
    rows_all = slab_rows * lax.axis_size("slab")
    probes_here = positions.shape[0]
    tall = slab_rows + 2 * HALO
    band = tall * cols
    highest = lax.Precision.HIGHEST
    weight_re, weight_im = beam_weights(amplitude, beam_index, positions, rows_all, cols)
    padded = padded_2(smatrix, (("slab", 2),), HALO)
    piece = lax.all_gather(padded, "probe", axis=1, tiled=True)
    count = piece.shape[1]
    flat = piece.reshape(2, count, band)
    real = jnp.dot(weight_re, flat[0], preferred_element_type=jnp.float32) - jnp.dot(
        weight_im, flat[1], preferred_element_type=jnp.float32
    )
    imag = jnp.dot(weight_re, flat[1], preferred_element_type=jnp.float32) + jnp.dot(
        weight_im, flat[0], preferred_element_type=jnp.float32
    )
    starts = positions[:, 0] + HALO
    wave_re = jax.vmap(lambda field, offset: cut_rows(field, offset, slab_rows))(
        real.reshape(probes_here, tall, cols), starts
    )
    wave_im = jax.vmap(lambda field, offset: cut_rows(field, offset, slab_rows))(
        imag.reshape(probes_here, tall, cols), starts
    )
    col_index = jnp.arange(cols, dtype=jnp.int32)
    col_cos, col_sin = dft_table(col_index, col_index, cols)
    half_re = jnp.dot(wave_re, col_cos, precision=highest) + jnp.dot(
        wave_im, col_sin, precision=highest
    )
    half_im = jnp.dot(wave_im, col_cos, precision=highest) - jnp.dot(
        wave_re, col_sin, precision=highest
    )
    scale = 1.0 / math.sqrt(rows_all * cols)
    local_rows = lax.axis_index("slab") * slab_rows + jnp.arange(slab_rows, dtype=jnp.int32)
    freq = jnp.arange(lax.axis_size("slab") * slab_rows, dtype=jnp.int32)
    row_cos, row_sin = dft_table(freq, local_rows, rows_all)
    out_re = jnp.einsum("kr,prc->kpc", row_cos, half_re, precision=highest) + jnp.einsum(
        "kr,prc->kpc", row_sin, half_im, precision=highest
    )
    out_im = jnp.einsum("kr,prc->kpc", row_cos, half_im, precision=highest) - jnp.einsum(
        "kr,prc->kpc", row_sin, half_re, precision=highest
    )
    summed = lax.psum_scatter(
        jnp.stack([out_re, out_im], 1) * scale, "slab", scatter_dimension=0, tiled=True
    )
    power = summed[:, 0] ** 2 + summed[:, 1] ** 2
    return jnp.transpose(power, (1, 0, 2))


def solution(mesh):
    return jax.shard_map(
        on_device,
        mesh=mesh,
        in_specs=(P(None, "probe", "slab", None), P(), P(), P("probe", None)),
        out_specs=P("probe", "slab", None),
        check_vma=False,
    )
```

profile of v0, /device:TPU:1, one launch (start us, length us, event | category | flops | bytes accessed | tf_op | source)
XLA Modules:
  0.0 566.4 jit_solution(1741276528891264881)
XLA Ops:
  6.5 0.0 all-gather.2.cloned.1.call-start
  6.5 0.8 fusion.116
  7.3 6.0 %collective-permute-start = (bf16[2,8,8,128]{3,2,1,0:T(8,128)(2,1)S(1)}, bf16[2,8,8,128]{3,2,1,0:T(8,128)(2,1)S(1)}, u32[]{:S(2)}, u32[]{:S(2)}) collective-permute-start(bf16[2,8,8,128]{3,2,1,0:T(8,128)(2,1)S(1)} %get-tuple-element.7), channel_id=1, source_target_pairs={{0,1},{1,2},{2,3},{4,5},{5,6},{6,7},{8,9},{9,10},{10,11},{12,13},{... | collective-permute-start | bytes 98312 | tf_op jit(solution)/shard_map/ppermute | solution.py:18
  13.3 1.9 collective-permute-start.1
  15.3 0.0 collective-permute-done
  15.3 4.8 collective-permute-done.1
  20.1 1.6 pad_maximum_fusion
  21.7 0.0 all-gather.2.cloned.1.call-update
  21.7 0.0 reduce-scatter.2.cloned.1.call-start
  21.8 0.8 or_bitcast_fusion
  22.5 0.8 fusion.117
  23.3 0.8 fusion.118
  24.1 276.4 %all-gather.2.cloned.1.call-done = bf16[2,512,48,128]{3,2,1,0:T(8,128)(2,1)} async-done(((bf16[2,8,48,128]{3,2,1,0:T(8,128)(2,1)}), bf16[2,512,48,128]{3,2,1,0:T(8,128)(2,1)}) %all-gather.2.cloned.1.call-update) | async-done | bytes 12582928 | tf_op jit(solution)/shard_map/all_gather | solution.py:60
  300.5 6.2 %fusion.115 = (bf16[1,512,48,128]{3,2,1,0:T(8,128)(2,1)S(1)}, bf16[1,512,48,128]{3,2,1,0:T(8,128)(2,1)S(1)}) fusion(bf16[2,512,48,128]{3,2,1,0:T(8,128)(2,1)} %all-gather.2.cloned.1.call-done), kind=kLoop, calls=%fused_computation.140 | loop fusion | bytes 25165824 | tf_op jit(solution)/shard_map/slice | solution.py:63
  306.7 2.4 fusion
  309.1 2.4 fusion.4
  311.4 2.6 fusion.21
  314.0 2.6 fusion.18
  316.6 2.0 copy.46
  318.7 0.4 copy.45
  319.1 6.3 %gather_fusion = f32[128,32,128]{2,0,1:T(8,128)} fusion(f32[128,48,128]{2,0,1:T(8,128)} %bitcast.71, s32[128]{0:T(128)S(1)} %get-tuple-element.13), kind=kCustom, calls=%fused_computation | custom fusion | bytes 4195840 | tf_op jit(solution)/shard_map/vmap()/gather | solution.py:47
  325.4 6.2 %gather_fusion.1 = f32[128,32,128]{2,0,1:T(8,128)} fusion(f32[128,48,128]{2,0,1:T(8,128)S(1)} %bitcast.70, s32[128]{0:T(128)S(1)} %get-tuple-element.13), kind=kCustom, calls=%fused_computation.1 | custom fusion | bytes 4195840 | tf_op jit(solution)/shard_map/vmap()/gather | solution.py:47
  331.6 0.0 copy-start.1
  331.6 3.9 fusion.37
  335.5 0.0 copy-done.1
  335.5 2.1 fusion.39
  337.7 0.0 copy-start
  337.7 2.1 convolution_subtract_fusion.1
  339.8 0.0 copy-done
  339.8 2.3 convolution_add_fusion.1
  342.1 7.4 %fusion.16 = f32[128,128,128]{2,0,1:T(8,128)S(1)} fusion(f32[128,32,128]{2,0,1:T(8,128)S(1)} %convolution_add_fusion.1, s32[32]{0:T(128)S(1)} %iota_add_fusion), kind=kOutput, calls=%fused_computation.27 | convolution fusion | flops 805363712 | bytes 10485888 | tf_op jit(solution)/shard_map/kr,prc->kpc/dot_general | solution.py:88
  349.5 7.7 %fusion.12 = f32[128,128,128]{2,0,1:T(8,128)S(1)} fusion(f32[128,32,128]{2,0,1:T(8,128)S(1)} %convolution_subtract_fusion.1, s32[32]{0:T(128)S(1)} %iota_add_fusion), kind=kOutput, calls=%fused_computation.23 | convolution fusion | flops 805363712 | bytes 10485888 | tf_op jit(solution)/shard_map/kr,prc->kpc/dot_general | solution.py:91
  357.2 7.4 %add_bitcast_fusion = f32[128,1,128,128]{3,0,2,1:T(8,128)S(1)} fusion(f32[128,128,128]{2,0,1:T(8,128)S(1)} %fusion.16, f32[128,32,128]{2,0,1:T(8,128)S(1)} %convolution_subtract_fusion.1, s32[32]{0:T(128)S(1)} %iota_add_fusion), kind=kOutput, calls=%fused_computation.4 | convolution fusion | flops 807460864 | bytes 18874496 | tf_op jit(solution)/shard_map/kr,prc->kpc/dot_general | solution.py:88
  364.6 7.7 %subtract_bitcast_fusion = f32[128,1,128,128]{3,0,2,1:T(8,128)S(1)} fusion(f32[128,128,128]{2,0,1:T(8,128)S(1)} %fusion.12, f32[128,32,128]{2,0,1:T(8,128)S(1)} %convolution_add_fusion.1, s32[32]{0:T(128)S(1)} %iota_add_fusion), kind=kOutput, calls=%fused_computation.3 | convolution fusion | flops 807460864 | bytes 18874496 | tf_op jit(solution)/shard_map/kr,prc->kpc/dot_general | solution.py:91
  372.3 6.0 %maximum_multiply_fusion = f32[128,2,128,128]{3,0,2,1:T(8,128)} fusion(f32[128,1,128,128]{3,0,2,1:T(8,128)S(1)} %subtract_bitcast_fusion, f32[128,1,128,128]{3,0,2,1:T(8,128)S(1)} %add_bitcast_fusion), kind=kLoop, calls=%fused_computation.2 | loop fusion | flops 8388608 | bytes 33554432 | tf_op jit(solution)/shard_map/mul | solution.py:95
  378.4 0.0 reduce-scatter.2.cloned.1.call-update
  378.4 176.7 %reduce-scatter.2.cloned.1.call-done = f32[32,2,128,128]{3,0,2,1:T(8,128)} async-done(((f32[128,2,128,128]{3,0,2,1:T(8,128)}), f32[32,2,128,128]{3,0,2,1:T(8,128)}) %reduce-scatter.2.cloned.1.call-update) | async-done | bytes 4194320 | tf_op jit(solution)/shard_map/reduce_scatter | solution.py:94
  555.1 4.0 fusion.11
  (1 shorter events, 0.0 us)
Async XLA Ops:
  6.5 294.0 %all-gather.2.cloned.1.call-start = ((), (), s32[]{:S(2)}) async-start(), calls=%async_computation.1 | async-start | bytes 12779520 | tf_op jit(solution)/shard_map/all_gather | solution.py:60
  7.3 8.0 %collective-permute-start = (bf16[2,8,8,128]{3,2,1,0:T(8,128)(2,1)S(1)}, bf16[2,8,8,128]{3,2,1,0:T(8,128)(2,1)S(1)}, u32[]{:S(2)}, u32[]{:S(2)}) collective-permute-start(bf16[2,8,8,128]{3,2,1,0:T(8,128)(2,1)S(1)} %get-tuple-element.7), channel_id=1, source_target_pairs={{0,1},{1,2},{2,3},{4,5},{5,6},{6,7},{8,9},{9,10},{10,11},{12,13},{... | collective-permute-start | bytes 98312 | tf_op jit(solution)/shard_map/ppermute | solution.py:18
  13.3 6.7 %collective-permute-start.1 = (bf16[2,8,8,128]{3,2,1,0:T(8,128)(2,1)S(1)}, bf16[2,8,8,128]{3,2,1,0:T(8,128)(2,1)S(1)}, u32[]{:S(2)}, u32[]{:S(2)}) collective-permute-start(bf16[2,8,8,128]{3,2,1,0:T(8,128)(2,1)S(1)} %get-tuple-element.8), channel_id=1, source_target_pairs={{1,0},{2,1},{3,2},{5,4},{6,5},{7,6},{9,8},{10,9},{11,10},{13,12},{... | collective-permute-start | bytes 98312 | tf_op jit(solution)/shard_map/ppermute | solution.py:19
  21.7 533.4 %reduce-scatter.2.cloned.1.call-start = ((), (), s32[]{:S(2)}) async-start(), calls=%async_computation.2 | async-start | bytes 20971520 | tf_op jit(solution)/shard_map/reduce_scatter | solution.py:94
  331.6 3.9 copy-start.1
  337.7 2.1 copy-start
Sparse Core Ops, SparseCore 0:
  21.8 278.6 all-gather.1
  378.5 176.5 reduce-scatter.1
where the time goes:
time: 576 us; the launch traced here: 566 us
  waiting for transfers between devices  458 us (80%)
  matrix products  50.5 us (9%)
  local copies, waits for them, and re-layouts  23.5 us (4%)
  between operations  14 us (2%)
  other arithmetic  12.5 us (2%)
  starting transfers between devices  7.98 us (1%)
    all_gather x1, waiting for transfers between devices, on_device(): piece = lax.all_gather(padded, 'probe', axis=1, tiled=True)  276 us
    reduce_scatter x1, waiting for transfers between devices, on_device(): lax.psum_scatter(jnp.stack([out_re, out_im], 1) * scale, 'slab', scatter_...  177 us
    gather x2, local copies, waits for them, and re-layouts, cut_rows(): return lax.dynamic_slice_in_dim(field, offset, count, 0)  12.6 us
  transfers between devices with their start and end apart: 4, of which 3 were waited for; matrix products, arithmetic and copies ran while one was open for 0% of the time, Pallas kernels for 0%

commit v1 on v0

v1 whole, which is shorter than its diff:
```python
import math

import jax
import jax.numpy as jnp
from jax import lax
from jax.sharding import PartitionSpec as P

HALO = 8
SIDE = 2 * HALO + 1
SPOTS = SIDE * SIDE


def dft_table(first, second, length):
    angle = (
        2.0
        * math.pi
        * (jnp.mod(first[:, None] * second[None, :], length).astype(jnp.float32) / length)
    )
    return (jnp.cos(angle), jnp.sin(angle))


def spot_weights(amplitude, beam_index, rows_all, cols):
    spot = jnp.arange(SPOTS, dtype=jnp.int32)
    row, col = spot // SIDE - HALO, spot % SIDE - HALO
    turn = jnp.mod(beam_index[:, 0:1] * row[None, :], rows_all).astype(jnp.float32) / rows_all
    turn = turn + jnp.mod(beam_index[:, 1:2] * col[None, :], cols).astype(jnp.float32) / cols
    cosine, sine = jnp.cos(2.0 * math.pi * turn), jnp.sin(2.0 * math.pi * turn)
    re, im = amplitude[0][:, None], amplitude[1][:, None]
    return (
        (re * cosine + im * sine).astype(jnp.bfloat16),
        (im * cosine - re * sine).astype(jnp.bfloat16),
    )


def on_device(smatrix, amplitude, beam_index, positions):
    _, beams_here, slab_rows, cols = smatrix.shape
    groups = lax.axis_size("probe")
    slabs = lax.axis_size("slab")
    rows_all = slab_rows * slabs
    own = cols // groups
    highest = lax.Precision.HIGHEST
    f32 = jnp.float32
    index = jnp.arange(cols, dtype=jnp.int32)
    cos, sin = dft_table(index, index, cols)
    cos, sin = cos / math.sqrt(cols), sin / math.sqrt(cols)
    s_re, s_im = smatrix[0].astype(f32), smatrix[1].astype(f32)
    mm = lambda a, b: jnp.einsum("lc,brc->lbr", a, b, precision=highest)
    half = jnp.stack([mm(cos, s_re) + mm(sin, s_im), mm(cos, s_im) - mm(sin, s_re)], 1)
    half = half.astype(jnp.bfloat16).reshape(groups, own, 2, beams_here, slab_rows)
    got = lax.all_to_all(half, "probe", split_axis=0, concat_axis=0, tiled=True)
    got = lax.all_gather(got, "slab", axis=0)
    got = jnp.transpose(got, (2, 0, 5, 3, 1, 4)).reshape(own, rows_all, 2, groups * beams_here)
    w_re, w_im = spot_weights(amplitude, beam_index, rows_all, cols)
    field = jnp.concatenate([got[:, :, 0], got[:, :, 1]], axis=-1)
    u_re = jnp.dot(field, jnp.concatenate([w_re, -w_im], 0), preferred_element_type=f32)
    u_im = jnp.dot(field, jnp.concatenate([w_im, w_re], 0), preferred_element_type=f32)
    row = jnp.arange(rows_all, dtype=jnp.int32)[:, None]
    shift = (jnp.arange(SPOTS, dtype=jnp.int32) // SIDE - HALO)[None, :]
    inside = (row >= shift) & (row < rows_all + shift)
    u_re = jnp.where(inside[None], u_re, 0.0)
    u_im = jnp.where(inside[None], u_im, 0.0)
    freq = lax.axis_index("slab") * slab_rows + jnp.arange(slab_rows, dtype=jnp.int32)
    rcos, rsin = dft_table(freq, row[:, 0], rows_all)
    rcos, rsin = rcos / math.sqrt(rows_all), rsin / math.sqrt(rows_all)
    mm = lambda a, b: jnp.einsum("kr,lrs->lks", a, b, precision=highest)
    out_re = mm(rcos, u_re) + mm(rsin, u_im)
    out_im = mm(rcos, u_im) - mm(rsin, u_re)
    power = (out_re**2 + out_im**2).astype(jnp.bfloat16)
    table = lax.all_gather(power, "probe", axis=0, tiled=True)
    spot = (positions[:, 0] + HALO) * SIDE + positions[:, 1] + HALO
    pick = (spot[:, None] == jnp.arange(SPOTS, dtype=jnp.int32)[None, :]).astype(jnp.bfloat16)
    return jnp.einsum("ps,lks->pkl", pick, table, preferred_element_type=f32)


def solution(mesh):
    return jax.shard_map(
        on_device,
        mesh=mesh,
        in_specs=(P(None, "probe", "slab", None), P(), P(), P("probe", None)),
        out_specs=P("probe", "slab", None),
        check_vma=False,
    )
```

time: 576 us -> 373 us (0.65)
  the two profiles are of different devices: /device:TPU:1 before, /device:TPU:4 now
where the time goes in v1:
time: 373 us; the launch traced here: 372 us
  waiting for transfers between devices  303 us (81%)
  blocking collectives  15.7 us (4%)
  between operations  13.6 us (4%)
  starting transfers between devices  12.8 us (3%)
  matrix products  12.7 us (3%)
  local copies, waits for them, and re-layouts  8.13 us (2%)
  other arithmetic  6.82 us (2%)
    all_gather x1, waiting for transfers between devices, on_device(): table = lax.all_gather(power, 'probe', axis=0, tiled=True)  299 us
    all_gather x1, blocking collectives, on_device(): got = lax.all_gather(got, 'slab', axis=0)  15.7 us
    all_to_all x1, starting transfers between devices, on_device(): got = lax.all_to_all(half, 'probe', split_axis=0, concat_axis=0, tiled=True)  12.7 us
  transfers between devices with their start and end apart: 2, of which 2 were waited for; matrix products, arithmetic and copies ran while one was open for 2% of the time, Pallas kernels for 0%

profile of v1, /device:TPU:4, one launch (start us, length us, event | category | flops | bytes accessed | tf_op | source)
XLA Modules:
  0.0 372.4 jit_solution(1641833828458793947)
XLA Ops:
  6.5 0.0 copy-start
  6.5 0.0 copy-start.1
  6.5 1.3 fusion.31
  7.9 1.3 fusion.37
  9.2 1.3 fusion.6
  10.5 1.3 fusion.5
  11.9 0.2 copy.21
  12.1 0.2 copy.22
  12.2 0.1 copy_bitcast_fusion.1
  12.4 1.1 reshape.91
  13.4 12.7 %all-to-all-start = ((bf16[64,2,512]{2,1,0:T(2,128)(2,1)}), bf16[64,2,512]{2,1,0:T(2,128)(2,1)S(1)}, u32[]{:S(2)}, u32[]{:S(2)}) async-start(bf16[64,2,512]{2,1,0:T(2,128)(2,1)} %reshape.91), calls=%async_computation | async-start | bytes 262144 | tf_op jit(solution)/shard_map/all_to_all | solution.py:50
  26.2 0.0 all-gather.3.cloned.1.call-start
  26.3 0.0 copy-done
  26.3 0.0 copy-done.1
  26.3 0.1 fusion.24
  26.5 3.6 fusion.126
  30.1 2.9 subtract_convert_fusion
  33.0 4.1 %all-to-all-done = bf16[64,2,512]{2,1,0:T(2,128)(2,1)S(1)} async-done(((bf16[64,2,512]{2,1,0:T(2,128)(2,1)}), bf16[64,2,512]{2,1,0:T(2,128)(2,1)S(1)}, u32[]{:S(2)}, u32[]{:S(2)}) %all-to-all-start) | async-done | bytes 131104 | tf_op jit(solution)/shard_map/all_to_all | solution.py:50
  37.1 0.3 reshape.92
  37.4 0.1 copy.24
  37.5 15.7 %all-gather = bf16[256,2,2,8,32]{4,3,2,1,0:T(8,128)(2,1)S(1)} all-gather(bf16[64,2,2,8,32]{4,3,2,1,0:T(8,128)(2,1)S(1)} %copy.24), channel_id=2, replica_groups=mesh['probe'=64,'slab'=4] {'slab'}, dimensions={0}, use_global_device_ids=true | all-gather | bytes 655360 | tf_op jit(solution)/shard_map/all_gather | solution.py:51
  53.2 2.7 copy.38
  55.9 1.1 reshape.82
  56.9 0.0 copy-start.3
  57.0 0.1 copy.30
  57.1 0.1 copy.31
  57.3 0.4 convolution_select_fusion
  57.7 0.2 copy-done.3
  57.9 0.0 copy-start.2
  57.9 0.4 convolution_select_fusion.1
  58.3 0.6 fusion.63
  58.9 0.6 fusion.61
  59.5 0.6 fusion.9
  60.1 1.2 fusion.11
  61.3 0.0 all-gather.3.cloned.1.call-update
  61.3 0.0 copy-done.2
  61.4 298.6 %all-gather.3.cloned.1.call-done = bf16[128,32,289]{2,1,0:T(8,128)(2,1)} async-done(((bf16[2,32,289]{2,1,0:T(8,128)(2,1)}), bf16[128,32,289]{2,1,0:T(8,128)(2,1)}) %all-gather.3.cloned.1.call-update) | async-done | bytes 2367504 | tf_op jit(solution)/shard_map/all_gather | solution.py:69
  359.9 3.6 fusion.2
  363.6 2.0 copy.29
  (7 shorter events, 0.1 us)
Async XLA Ops:
  6.5 19.8 %copy-start = (f32[2,512]{1,0:T(2,128)S(1)}, f32[2,512]{1,0:T(2,128)}, u32[]{:S(2)}) copy-start(f32[2,512]{1,0:T(2,128)} %param.5) | copy-start | bytes 12292
  6.5 19.8 %copy-start.1 = (s32[512,2]{0,1:T(2,128)S(1)}, s32[512,2]{0,1:T(2,128)}, u32[]{:S(2)}) copy-start(s32[512,2]{0,1:T(2,128)} %param.6) | copy-start | bytes 12292
  13.4 23.7 %all-to-all-start = ((bf16[64,2,512]{2,1,0:T(2,128)(2,1)}), bf16[64,2,512]{2,1,0:T(2,128)(2,1)S(1)}, u32[]{:S(2)}, u32[]{:S(2)}) async-start(bf16[64,2,512]{2,1,0:T(2,128)(2,1)} %reshape.91), calls=%async_computation | async-start | bytes 262144 | tf_op jit(solution)/shard_map/all_to_all | solution.py:50
  26.2 333.8 %all-gather.3.cloned.1.call-start = ((), (), s32[]{:S(2)}) async-start(), calls=%async_computation.1 | async-start | bytes 3194880 | tf_op jit(solution)/shard_map/all_gather | solution.py:69
  56.9 1.0 copy-start.3
  57.9 3.5 copy-start.2
Sparse Core Ops, SparseCore 0:
  61.5 298.4 all-gather.2

commit v2 on v1

v2 whole, which is shorter than its diff:
```python
import functools
import math

import jax
import jax.numpy as jnp
import ml_dtypes
import numpy as np
from jax import lax
from jax.experimental import pallas as pl
from jax.experimental.pallas import tpu as pltpu
from jax.sharding import PartitionSpec as P

HALO = 8
SIDE = 2 * HALO + 1
SPOTS = 304
LANES = 384
QUAD = 4
MESH = pl.DeviceIdType.MESH
F32 = jnp.float32
BF16 = jnp.bfloat16


def two_terms(table):
    high = table.astype(ml_dtypes.bfloat16)
    low = (table - high.astype(np.float64)).astype(ml_dtypes.bfloat16)
    return np.stack([high, low])


def column_table(near, deep, cols):
    chip = np.arange(cols)
    far, probe = chip // (near * deep), chip % (near * deep)
    freq = (far * near + probe % near) * deep + probe // near
    turn = 2.0 * np.pi * ((freq[:, None] * np.arange(cols)[None, :]) % cols) / cols
    cos, sin = np.cos(turn), np.sin(turn)
    return two_terms(np.block([[cos, sin], [-sin, cos]]))


def row_table(slab_rows, slabs):
    length = slab_rows * slabs
    tables = []
    for core in range(2):
        freq = np.concatenate(
            [(far * 2 + core) * slab_rows + np.arange(slab_rows) for far in range(2)]
        )
        row = np.concatenate(
            [
                np.tile((far * 2 + side) * slab_rows + np.arange(slab_rows), QUAD)
                for side in (core, 1 - core)
                for far in range(2)
            ]
        )
        turn = 2.0 * np.pi * ((freq[:, None] * row[None, :]) % length) / length
        cos, sin = np.cos(turn), np.sin(turn)
        tables.append(two_terms(np.block([[cos, sin], [-sin, cos]])))
    return np.stack(tables)


def nt(a, b):
    return lax.dot_general(a, b, (((1,), (1,)), ((), ())), preferred_element_type=F32)


def unit_circle(turn):
    turn = turn - jnp.floor(turn + 0.5)
    quarter = jnp.floor(4.0 * turn + 0.5)
    phi = (2.0 * math.pi) * (turn - 0.25 * quarter)
    sq = phi * phi
    s = phi * (1.0 + sq * (-1.0 / 6 + sq * (1.0 / 120 + sq * (-1.0 / 5040 + sq / 362880))))
    c = 1.0 + sq * (-0.5 + sq * (1.0 / 24 + sq * (-1.0 / 720 + sq / 40320)))
    odd = jnp.abs(quarter) == 1.0
    a = jnp.where(odd, s, c)
    b = jnp.where(odd, c, s)
    cos_neg = (quarter == 1.0) | (jnp.abs(quarter) == 2.0)
    sin_neg = (quarter == -1.0) | (jnp.abs(quarter) == 2.0)
    return jnp.where(cos_neg, -a, a), jnp.where(sin_neg, -b, b)


def spot_offsets(width):
    spot = lax.broadcasted_iota(jnp.int32, (SPOTS, width), 0).astype(F32)
    row = jnp.floor((spot + 0.5) * (1.0 / SIDE))
    return row - HALO, spot - SIDE * row - HALO


def exchange(
    near, deep, slab_rows,
    s_ref, beam_ref, spot_ref, ctab_hbm, rtab_hbm, out_hbm,
    ctab, rtab, sendf, send, field, other, weight, high, low, planes, mixed, picks, spots, blocks,
    ctab_sem, rtab_sem, send_sem, recv_sem, pair_send, pair_recv,
    deep_send, deep_recv, spot_send, spot_recv, near_send, near_recv, keep_sem,
):
    probe, slab = lax.axis_index("probe"), lax.axis_index("slab")
    probes = near * deep
    chips = 2 * probes
    wide = 2 * near
    far, core = slab // 2, slab % 2
    chip = far * probes + probe
    z, flat = probe // near, probe % near
    here = far * near + flat

    def device(index):
        return (index % probes, (index // probes) * 2 + core)

    pair = (probe, far * 2 + 1 - core)
    barrier = pltpu.get_barrier_semaphore()

    @pl.loop(1, chips)
    def _(i):
        pl.semaphore_signal(barrier, inc=1, device_id=device((chip + i) % chips), device_id_type=MESH)

    pl.semaphore_signal(barrier, inc=1, device_id=pair, device_id_type=MESH)
    ctab_copy = pltpu.make_async_copy(ctab_hbm, ctab, ctab_sem)
    ctab_copy.start()
    rtab_copy = pltpu.make_async_copy(rtab_hbm.at[core], rtab, rtab_sem)
    rtab_copy.start()

    ctab_copy.wait()
    both = jnp.concatenate([s_ref[0], s_ref[1]], axis=1)
    half = nt(ctab[0], both) + nt(ctab[1], both)
    lanes = QUAD * slab_rows
    for part in range(2):
        for h in range(2):
            sendf[pl.ds(part * 2 + h, chips, stride=4), :] = half[
                part * chips : (part + 1) * chips, h * lanes : (h + 1) * lanes
            ]
    send[...] = sendf[...].astype(BF16).reshape(chips, 4, lanes)
    spots[flat] = spot_ref[...]
    pl.semaphore_wait(barrier, chips)

    @pl.loop(1, chips)
    def _(i):
        to = (chip + i) % chips
        pltpu.make_async_remote_copy(
            src_ref=send.at[to], dst_ref=field.at[chip], send_sem=send_sem, recv_sem=recv_sem,
            device_id=device(to), device_id_type=MESH,
        ).start()

    pltpu.make_async_copy(send.at[chip], field.at[chip], recv_sem).start()
    spot_copies = []
    for i in range(1, near):
        copy = pltpu.make_async_remote_copy(
            src_ref=spot_ref, dst_ref=spots.at[flat], send_sem=spot_send.at[i],
            recv_sem=spot_recv.at[flat], device_id=(z * near + (flat + i) % near, slab),
            device_id_type=MESH,
        )
        copy.start()
        spot_copies.append(copy)

    kdim = weight.shape[1]
    r0, c0 = spot_offsets(kdim)
    for j in range(QUAD):
        turn = (beam_ref[j : j + 1, :] * r0 + beam_ref[4 + j : 5 + j, :] * c0) * (
            1.0 / (4 * slab_rows)
        )
        cos, sin = unit_circle(turn)
        re, im = beam_ref[8 + j : 9 + j, :], beam_ref[12 + j : 13 + j, :]
        weight[j * SPOTS : (j + 1) * SPOTS, :] = (re * cos + im * sin).astype(BF16)
        weight[(4 + j) * SPOTS : (5 + j) * SPOTS, :] = (im * cos - re * sin).astype(BF16)
    planes[z] = jnp.zeros(planes.shape[1:], BF16)

    pltpu.make_async_copy(field, field, recv_sem).wait()
    swap = pltpu.make_async_remote_copy(
        src_ref=field, dst_ref=other, send_sem=pair_send, recv_sem=pair_recv,
        device_id=pair, device_id_type=MESH,
    )
    swap.start()

    def beam_sum(source, side, turn):
        r0, _ = spot_offsets(2 * lanes)
        lane = lax.broadcasted_iota(jnp.int32, (SPOTS, 2 * lanes), 1)
        group = (lane % lanes) // slab_rows
        row = ((lane // lanes) * 2 + side) * slab_rows + lane % slab_rows
        rowf = row.astype(F32)
        inside = (rowf >= r0) & (rowf < r0 + 4.0 * slab_rows)
        x = jnp.concatenate(
            [
                source[0:probes].reshape(probes * 4, lanes),
                source[probes : 2 * probes].reshape(probes * 4, lanes),
            ],
            axis=1,
        )
        for part in range(2):
            total = None
            for j in range(QUAD):
                w = weight[(part * QUAD + j) * SPOTS : (part * QUAD + j + 1) * SPOTS, :]
                y = jnp.dot(w, x, preferred_element_type=F32)
                total = y if j == 0 else jnp.where(group == j, y, total)
            total = jnp.where(inside, total, 0.0)
            top = total.astype(BF16)
            at = (part * 2 + turn) * 2 * lanes
            high[:, at : at + 2 * lanes] = top
            low[:, at : at + 2 * lanes] = (total - top.astype(F32)).astype(BF16)

    beam_sum(field, core, 0)
    for i in range(near):
        at = (flat + i) % near
        if i > 0:
            pltpu.make_async_remote_copy(
                src_ref=spot_ref, dst_ref=spots.at[at], send_sem=spot_send.at[i],
                recv_sem=spot_recv.at[at], device_id=pair, device_id_type=MESH,
            ).wait_recv()
        width = spot_ref.shape[1]
        index = spots[at][0:1, :]
        row = lax.broadcasted_iota(jnp.int32, (SPOTS, width), 0).astype(F32)
        picks[:, i * width : (i + 1) * width] = jnp.where(row == index, 1.0, 0.0).astype(BF16)
    swap.wait_recv()
    beam_sum(other, 1 - core, 1)
    rtab_copy.wait()
    out = nt(rtab[0], high[...]) + (nt(rtab[0], low[...]) + nt(rtab[1], high[...]))
    count = 2 * slab_rows
    re, im = out[:count], out[count:]
    scale = 1.0 / (4 * slab_rows * chips)
    power = (re * re + im * im) * scale
    planes[z, :, 0:SPOTS] = power.astype(BF16)

    def deep_copy(i, slot):
        return pltpu.make_async_remote_copy(
            src_ref=planes.at[slot], dst_ref=planes.at[slot], send_sem=deep_send.at[i],
            recv_sem=deep_recv.at[slot], device_id=(((z + i) % deep) * near + flat, slab),
            device_id_type=MESH,
        )

    order = sorted(range(1, deep), key=lambda i: (min(i, deep - i), i))
    for i in order:
        deep_copy(i, z).start()
    for i in [0] + order:
        slot = (z + i) % deep
        if i > 0:
            deep_copy(i, slot).wait_recv()
        plane = planes[slot].astype(F32)
        for t in range(LANES // 128):
            mixed[t, pl.ds(slot, count, stride=deep), :] = plane[:, t * 128 : (t + 1) * 128]

    left = jnp.concatenate([mixed[t] for t in range(LANES // 128)], axis=1)
    left = left[:, 0:SPOTS].astype(BF16)
    rows = slab_rows * deep
    width = spot_ref.shape[1]

    def near_copy(i, target, to, slot):
        return pltpu.make_async_remote_copy(
            src_ref=blocks.at[i, target], dst_ref=out_hbm.at[slot],
            send_sem=near_send.at[i, target], recv_sem=near_recv.at[slot],
            device_id=(z * near + (to % near), target * 2 + core), device_id_type=MESH,
        )

    for i in range(0, near, 2):
        got = jnp.dot(
            left, picks[:, i * width : (i + 2) * width], preferred_element_type=F32
        ).astype(BF16)
        for d in range(2):
            for target in range(2):
                blocks[i + d, target] = got[
                    target * rows : (target + 1) * rows, d * width : (d + 1) * width
                ]
            if i + d == 0:
                near_copy(0, 1 - far, flat, here).start()
            else:
                for target in range(2):
                    near_copy(i + d, target, flat + i + d, here).start()
    keep = pltpu.make_async_copy(blocks.at[0, far], out_hbm.at[here], keep_sem)
    keep.start()
    keep.wait()
    for i in range(near):
        for target in range(2):
            if i == 0:
                continue
            copy = near_copy(i, target, flat + i, target * near + (flat + i) % near)
            copy.wait()
    copy = near_copy(0, 1 - far, flat, (1 - far) * near + flat)
    copy.wait()
    for i in order:
        deep_copy(i, z).wait_send()
    for copy in spot_copies:
        copy.wait_send()
    swap.wait_send()
    gone = send.at[pl.ds(0, chips - 1)]
    pltpu.make_async_copy(gone, gone, send_sem).wait()


def to_columns(deep, in_ref, out_ref):
    wide, rows, probes = in_ref.shape
    count = rows // deep
    for k in range(0, count, 2):
        pairs = in_ref[:, k * deep : (k + 2) * deep, :].astype(F32)
        for e in range(2):
            block = pairs[:, e * deep : (e + 1) * deep, :].reshape(wide * deep, probes)
            out_ref[:, k + e, :] = block.T


def on_device(smatrix, amplitude, beam_index, positions):
    _, beams_here, slab_rows, cols = smatrix.shape
    probes = lax.axis_size("probe")
    near = 8 if probes == 64 else 2
    deep = probes // near
    wide = 2 * near
    chips = 2 * probes
    slabs = lax.axis_size("slab")
    probes_here = positions.shape[0]
    lanes = QUAD * slab_rows
    kdim = 4 * probes
    split = lambda v: jnp.transpose(v.reshape(probes, 2, QUAD), (2, 0, 1))[:, :, None, :]
    twice = lambda a, b: jnp.concatenate([split(a), split(b)], 2).reshape(QUAD, kdim)
    freq = beam_index.astype(F32)
    beam = jnp.concatenate(
        [
            twice(freq[:, 0], freq[:, 0]),
            twice(freq[:, 1], freq[:, 1]),
            twice(amplitude[0], -amplitude[1]),
            twice(amplitude[1], amplitude[0]),
        ],
        0,
    )
    spot = ((positions[:, 0] + HALO) * SIDE + positions[:, 1] + HALO).astype(F32)
    spot = jnp.broadcast_to(spot[None, :], (8, probes_here))
    ctab = jnp.asarray(column_table(near, deep, cols))
    rtab = jnp.asarray(row_table(slab_rows, slabs))
    vmem = pl.BlockSpec(memory_space=pltpu.VMEM)
    hbm = pl.BlockSpec(memory_space=pl.ANY)
    dma = pltpu.SemaphoreType.DMA
    picked = pl.pallas_call(
        functools.partial(exchange, near, deep, slab_rows),
        out_shape=jax.ShapeDtypeStruct((wide, slab_rows * deep, probes_here), BF16),
        in_specs=[vmem, vmem, vmem, hbm, hbm],
        out_specs=hbm,
        scratch_shapes=[
            pltpu.VMEM(ctab.shape, BF16),
            pltpu.VMEM(rtab.shape[1:], BF16),
            pltpu.VMEM((chips * 4, lanes), F32),
            pltpu.VMEM((chips, 4, lanes), BF16),
            pltpu.VMEM((chips, 4, lanes), BF16),
            pltpu.VMEM((chips, 4, lanes), BF16),
            pltpu.VMEM((2 * QUAD * SPOTS, kdim), BF16),
            pltpu.VMEM((SPOTS, 8 * lanes), BF16),
            pltpu.VMEM((SPOTS, 8 * lanes), BF16),
            pltpu.VMEM((deep, 2 * slab_rows, LANES), BF16),
            pltpu.VMEM((LANES // 128, 2 * slab_rows * deep, 128), F32),
            pltpu.VMEM((SPOTS, near * probes_here), BF16),
            pltpu.VMEM((near, 8, probes_here), F32),
            pltpu.VMEM((near, 2, slab_rows * deep, probes_here), BF16),
            dma, dma, dma, dma, dma, dma,
            dma((deep,)), dma((deep,)), dma((near,)), dma((near,)),
            dma((near, 2)), dma((wide,)), dma,
        ],
        compiler_params=pltpu.CompilerParams(
            collective_id=0, has_side_effects=True, vmem_limit_bytes=48 * 1024 * 1024
        ),
    )(smatrix.reshape(2, beams_here * slab_rows, cols), beam, spot, ctab, rtab)
    step = min(8, slab_rows)
    return pl.pallas_call(
        functools.partial(to_columns, deep),
        grid=(slab_rows // step,),
        in_specs=[pl.BlockSpec((wide, step * deep, probes_here), lambda i: (0, i, 0))],
        out_specs=pl.BlockSpec((probes_here, step, cols), lambda i: (0, i, 0)),
        out_shape=jax.ShapeDtypeStruct((probes_here, slab_rows, cols), F32),
    )(picked)


def solution(mesh):
    return jax.shard_map(
        on_device,
        mesh=mesh,
        in_specs=(P(None, "probe", "slab", None), P(), P(), P("probe", None)),
        out_specs=P("probe", "slab", None),
        check_vma=False,
    )
```

time: 373 us -> 61.5 us (0.16)
  the two profiles are of different devices: /device:TPU:4 before, /device:TPU:1 now
where the time goes in v2:
time: 61.5 us; the launch traced here: 61.3 us
  Pallas kernels  56.5 us (92%)
  local copies, waits for them, and re-layouts  2.87 us (5%)
  other arithmetic  1.78 us (3%)
    pallas_call x1, Pallas kernels, on_device(): pl.pallas_call(functools.partial(exchange, near, deep, slab_rows), out_sh...  52.2 us
    pallas_call x1, Pallas kernels, on_device(): pl.pallas_call(functools.partial(to_columns, deep), grid=(slab_rows // st...  4.22 us

profile of v2, /device:TPU:1, one launch (start us, length us, event | category | flops | bytes accessed | tf_op | source)
XLA Modules:
  0.0 61.3 jit_solution(10552364884347871990)
XLA Ops:
  0.0 0.0 copy-start.1
  0.0 0.0 copy-start.2
  0.0 0.0 copy-start.3
  0.0 0.8 %convert_bitcast_fusion = f32[128]{0:T(128)S(1)} fusion(s32[128,2]{0,1:T(2,128)} %param.9), kind=kLoop, calls=%fused_computation.10 | loop fusion | flops 640 | bytes 1536 | tf_op jit(solution)/shard_map/convert_element_type | solution.py:311
  0.8 0.7 %convert_element_type.10 = f32[512,2]{0,1:T(2,128)S(1)} convert(s32[512,2]{0,1:T(2,128)} %param.8) | non-fusion elementwise | flops 1024 | bytes 8192 | tf_op jit(solution)/shard_map/convert_element_type | solution.py:301
  1.5 0.8 %slice_reduce_fusion.2 = (f32[512]{0:T(512)S(1)}, f32[512]{0:T(512)S(1)}) fusion(f32[2,512]{1,0:T(2,128)} %param.7), kind=kLoop, calls=%fused_computation.8 | loop fusion | bytes 8192 | tf_op jit(solution)/shard_map/slice | solution.py:306
  2.3 0.1 squeeze.2
  2.5 0.1 reshape_squeeze.6
  2.7 0.1 copy.40
  2.9 0.1 reshape_squeeze.15
  3.0 0.1 reshape_squeeze.14
  3.3 0.1 copy.41
  3.3 0.1 pad_maximum_fusion.2
  3.5 0.1 copy.42
  3.6 0.1 copy.39
  3.7 0.1 copy.43
  3.8 0.0 copy-done.1
  3.8 0.0 copy-done.2
  3.8 0.0 copy-done.3
  3.8 52.2 %shard_map.64.in_ref = bf16[16,256,128]{2,1,0:T(8,128)(2,1)S(1)} custom-call(bf16[2,256,128]{2,1,0:T(8,128)(2,1)S(1)} %bitcast.23, f32[16,256]{1,0:T(8,128)S(1)} %pad_maximum_fusion.4.beam_ref, f32[8,128]{1,0:T(8,128)S(1)} %broadcast_in_dim.29.spot_ref, bf16[2,256,256]{2,1,0:T(8,128)(2,1)S(1)} %copy-done.2, bf16[2,2,128,1024]{3,2,1,0:T(8,128)(2,1)S(1)} %copy-done.1), custom_call_target="tpu_custom_call" | custom-call | tf_op jit(solution)/shard_map/pallas_call | solution.py:318
  56.1 0.0 copy-start
  56.1 1.0 %copy-done = bf16[16,256,128]{2,1,0:T(8,128)(2,1)} copy-done((bf16[16,256,128]{2,1,0:T(8,128)(2,1)}, bf16[16,256,128]{2,1,0:T(8,128)(2,1)S(1)}, u32[]{:S(2)}) %copy-start) | copy-done | bytes 1048600
  57.1 4.2 %shard_map.65 = f32[128,32,128]{2,1,0:T(8,128)} custom-call(bf16[16,256,128]{2,1,0:T(8,128)(2,1)} %copy-done), custom_call_target="tpu_custom_call" | custom-call | tf_op jit(solution)/shard_map/pallas_call | solution.py:347
  (9 shorter events, 0.3 us)
Async XLA Ops:
  0.0 3.8 %copy-start.1 = (bf16[2,2,128,1024]{3,2,1,0:T(8,128)(2,1)S(1)}, bf16[2,2,128,1024]{3,2,1,0:T(8,128)(2,1)}, u32[]{:S(2)}) copy-start(bf16[2,2,128,1024]{3,2,1,0:T(8,128)(2,1)} %constant.9.clone.rtab_hbm) | copy-start | bytes 3145732
  0.0 3.8 %copy-start.2 = (bf16[2,256,256]{2,1,0:T(8,128)(2,1)S(1)}, bf16[2,256,256]{2,1,0:T(8,128)(2,1)}, u32[]{:S(2)}) copy-start(bf16[2,256,256]{2,1,0:T(8,128)(2,1)} %constant.8.clone.ctab_hbm) | copy-start | bytes 786436
  0.0 3.8 %copy-start.3 = (bf16[2,8,32,128]{3,2,1,0:T(8,128)(2,1)S(1)}, bf16[2,8,32,128]{3,2,1,0:T(8,128)(2,1)}, u32[]{:S(2)}) copy-start(bf16[2,8,32,128]{3,2,1,0:T(8,128)(2,1)} %param.6) | copy-start | bytes 393220
  56.1 1.0 %copy-start = (bf16[16,256,128]{2,1,0:T(8,128)(2,1)}, bf16[16,256,128]{2,1,0:T(8,128)(2,1)S(1)}, u32[]{:S(2)}) copy-start(bf16[16,256,128]{2,1,0:T(8,128)(2,1)S(1)} %shard_map.64.in_ref) | copy-start | bytes 3145732

commit v3 on v2

v3 whole, which is shorter than its diff:
```python
import functools
import math

import jax
import jax.numpy as jnp
import ml_dtypes
import numpy as np
from jax import lax
from jax.experimental import pallas as pl
from jax.experimental.pallas import tpu as pltpu
from jax.sharding import PartitionSpec as P

HALO = 8
SIDE = 2 * HALO + 1
SPOTS = 304
QUAD = 4
MESH = pl.DeviceIdType.MESH
F32 = jnp.float32
BF16 = jnp.bfloat16


def two_terms(table):
    high = table.astype(ml_dtypes.bfloat16)
    low = (table - high.astype(np.float64)).astype(ml_dtypes.bfloat16)
    return np.stack([high, low])


def column_table(near, deep, cols):
    chip = np.arange(cols)
    far, probe = chip // (near * deep), chip % (near * deep)
    freq = (far * near + probe % near) * deep + probe // near
    turn = 2.0 * np.pi * ((freq[:, None] * np.arange(cols)[None, :]) % cols) / cols
    cos, sin = np.cos(turn), np.sin(turn)
    return two_terms(np.block([[cos, sin], [-sin, cos]]))


def row_table(slab_rows, slabs):
    length = slab_rows * slabs
    tables = []
    for core in range(2):
        freq = np.concatenate(
            [(far * 2 + core) * slab_rows + np.arange(slab_rows) for far in range(2)]
        )
        row = np.concatenate(
            [
                np.tile((far * 2 + side) * slab_rows + np.arange(slab_rows), QUAD)
                for side in (core, 1 - core)
                for far in range(2)
            ]
        )
        turn = 2.0 * np.pi * ((freq[:, None] * row[None, :]) % length) / length
        cos, sin = np.cos(turn), np.sin(turn)
        tables.append(two_terms(np.block([[cos, sin], [-sin, cos]])))
    return np.stack(tables)


def nt(a, b):
    return lax.dot_general(a, b, (((1,), (1,)), ((), ())), preferred_element_type=F32)


def unit_circle(turn):
    turn = turn - jnp.floor(turn + 0.5)
    quarter = jnp.floor(4.0 * turn + 0.5)
    phi = (2.0 * math.pi) * (turn - 0.25 * quarter)
    sq = phi * phi
    s = phi * (1.0 + sq * (-1.0 / 6 + sq * (1.0 / 120 + sq * (-1.0 / 5040 + sq / 362880))))
    c = 1.0 + sq * (-0.5 + sq * (1.0 / 24 + sq * (-1.0 / 720 + sq / 40320)))
    odd = jnp.abs(quarter) == 1.0
    a = jnp.where(odd, s, c)
    b = jnp.where(odd, c, s)
    cos_neg = (quarter == 1.0) | (jnp.abs(quarter) == 2.0)
    sin_neg = (quarter == -1.0) | (jnp.abs(quarter) == 2.0)
    return jnp.where(cos_neg, -a, a), jnp.where(sin_neg, -b, b)


def spot_offsets(width):
    spot = lax.broadcasted_iota(jnp.int32, (SPOTS, width), 0).astype(F32)
    row = jnp.floor((spot + 0.5) * (1.0 / SIDE))
    return row - HALO, spot - SIDE * row - HALO


def beam_rows(amp_ref, freq_ref, probes):
    kdim = 4 * probes
    beams = amp_ref.shape[1]
    rows = [freq_ref[0:1, :].astype(F32), freq_ref[1:2, :].astype(F32)]
    for part in range(2):
        rest = amp_ref[part : part + 1, :]
        for _ in range(3):
            piece = rest.astype(BF16).astype(F32)
            rows.append(piece)
            rest = rest - piece
    stack = jnp.concatenate(rows, axis=0).astype(BF16)
    beam = lax.broadcasted_iota(jnp.int32, (beams, QUAD * kdim), 0)
    lane = lax.broadcasted_iota(jnp.int32, (beams, QUAD * kdim), 1)
    j, k = lane // kdim, lane % kdim
    pick = beam == (k // 4) * 8 + (k % 2) * QUAD + j
    got = jnp.dot(stack, jnp.where(pick, 1.0, 0.0).astype(BF16), preferred_element_type=F32)
    re = got[2:3] + got[3:4] + got[4:5]
    im = got[5:6] + got[6:7] + got[7:8]
    second = (lax.broadcasted_iota(jnp.int32, (1, QUAD * kdim), 1) // 2) % 2 == 1
    return got[0:1], got[1:2], jnp.where(second, -im, re), jnp.where(second, re, im)


def exchange(
    near, deep,
    s_ref, amp_ref, freq_ref, place_ref, ctab_hbm, rtab_hbm, out_ref,
    ctab, rtab, sendf, send, field, other, weight, high, low, planes, picks, spot, spots,
    blocks, landed, wide_f,
    ctab_sem, rtab_sem, send_sem, recv_sem, pair_send, pair_recv,
    deep_send, deep_recv, spot_send, spot_recv, near_send, near_recv,
):
    probe, slab = lax.axis_index("probe"), lax.axis_index("slab")
    _, beams_here, slab_rows, cols = s_ref.shape
    probes = near * deep
    chips = 2 * probes
    wide = 2 * near
    far, core = slab // 2, slab % 2
    chip = far * probes + probe
    z, flat = probe // near, probe % near
    here = far * near + flat

    def device(index):
        return (index % probes, (index // probes) * 2 + core)

    pair = (probe, far * 2 + 1 - core)
    barrier = pltpu.get_barrier_semaphore()

    @pl.loop(1, chips)
    def _(i):
        pl.semaphore_signal(barrier, inc=1, device_id=device((chip + i) % chips), device_id_type=MESH)

    pl.semaphore_signal(barrier, inc=1, device_id=pair, device_id_type=MESH)
    ctab_copy = pltpu.make_async_copy(ctab_hbm, ctab, ctab_sem)
    ctab_copy.start()
    rtab_copy = pltpu.make_async_copy(rtab_hbm.at[core], rtab, rtab_sem)
    rtab_copy.start()
    width = place_ref.shape[1]
    index = (place_ref[0:1, :] + HALO) * SIDE + place_ref[1:2, :] + HALO
    spot[...] = jnp.broadcast_to(index.astype(F32), (8, width))

    ctab_copy.wait()
    parts = [s_ref[part].reshape(beams_here * slab_rows, cols) for part in range(2)]
    both = jnp.concatenate(parts, axis=1)
    half = nt(ctab[0], both) + nt(ctab[1], both)
    lanes = QUAD * slab_rows
    for part in range(2):
        for h in range(2):
            sendf[pl.ds(part * 2 + h, chips, stride=4), :] = half[
                part * chips : (part + 1) * chips, h * lanes : (h + 1) * lanes
            ]
    send[...] = sendf[...].astype(BF16).reshape(chips, 4, lanes)
    spots[flat] = spot[...]
    pl.semaphore_wait(barrier, chips)

    @pl.loop(1, chips)
    def _(i):
        to = (chip + i) % chips
        pltpu.make_async_remote_copy(
            src_ref=send.at[to], dst_ref=field.at[chip], send_sem=send_sem, recv_sem=recv_sem,
            device_id=device(to), device_id_type=MESH,
        ).start()

    pltpu.make_async_copy(send.at[chip], field.at[chip], recv_sem).start()
    spot_copies = []
    for i in range(1, near):
        copy = pltpu.make_async_remote_copy(
            src_ref=spot, dst_ref=spots.at[flat], send_sem=spot_send.at[i],
            recv_sem=spot_recv.at[flat], device_id=(z * near + (flat + i) % near, slab),
            device_id_type=MESH,
        )
        copy.start()
        spot_copies.append(copy)

    kdim = weight.shape[1]
    f0, f1, amp_re, amp_im = beam_rows(amp_ref, freq_ref, probes)
    r0, c0 = spot_offsets(kdim)
    for j in range(QUAD):
        at = slice(j * kdim, (j + 1) * kdim)
        cos, sin = unit_circle((f0[:, at] * r0 + f1[:, at] * c0) * (1.0 / (4 * slab_rows)))
        re, im = amp_re[:, at], amp_im[:, at]
        weight[j * SPOTS : (j + 1) * SPOTS, :] = (re * cos + im * sin).astype(BF16)
        weight[(4 + j) * SPOTS : (5 + j) * SPOTS, :] = (im * cos - re * sin).astype(BF16)

    pltpu.make_async_copy(field, field, recv_sem).wait()
    swap = pltpu.make_async_remote_copy(
        src_ref=field, dst_ref=other, send_sem=pair_send, recv_sem=pair_recv,
        device_id=pair, device_id_type=MESH,
    )
    swap.start()

    def beam_sum(source, side, turn):
        r0, _ = spot_offsets(2 * lanes)
        lane = lax.broadcasted_iota(jnp.int32, (SPOTS, 2 * lanes), 1)
        group = (lane % lanes) // slab_rows
        row = ((lane // lanes) * 2 + side) * slab_rows + lane % slab_rows
        rowf = row.astype(F32)
        inside = (rowf >= r0) & (rowf < r0 + 4.0 * slab_rows)
        x = jnp.concatenate(
            [
                source[0:probes].reshape(probes * 4, lanes),
                source[probes : 2 * probes].reshape(probes * 4, lanes),
            ],
            axis=1,
        )
        for part in range(2):
            total = None
            for j in range(QUAD):
                w = weight[(part * QUAD + j) * SPOTS : (part * QUAD + j + 1) * SPOTS, :]
                y = jnp.dot(w, x, preferred_element_type=F32)
                total = y if j == 0 else jnp.where(group == j, y, total)
            total = jnp.where(inside, total, 0.0)
            top = total.astype(BF16)
            at = (part * 2 + turn) * 2 * lanes
            high[:, at : at + 2 * lanes] = top
            low[:, at : at + 2 * lanes] = (total - top.astype(F32)).astype(BF16)

    beam_sum(field, core, 0)
    for i in range(near):
        at = (flat + i) % near
        if i > 0:
            pltpu.make_async_remote_copy(
                src_ref=spot, dst_ref=spots.at[at], send_sem=spot_send.at[i],
                recv_sem=spot_recv.at[at], device_id=pair, device_id_type=MESH,
            ).wait_recv()
        row = lax.broadcasted_iota(jnp.int32, (384, width), 0)
        row = jnp.where(row >= 320, row - 64, row).astype(F32)
        hit = row == spots[at][0:1, :]
        picks[:, i * width : (i + 1) * width] = jnp.where(hit, 1.0, 0.0).astype(BF16)
    swap.wait_recv()
    beam_sum(other, 1 - core, 1)
    rtab_copy.wait()
    out = nt(rtab[0], high[...]) + (nt(rtab[0], low[...]) + nt(rtab[1], high[...]))
    count = 2 * slab_rows
    re, im = out[:count], out[count:]
    scale = 1.0 / (4 * slab_rows * chips)
    power = ((re * re + im * im) * scale).astype(BF16)
    rest = jnp.concatenate([power[:, 256:SPOTS], jnp.zeros((count, 320 - SPOTS), BF16)], axis=1)
    planes[z, 0:count] = power[:, 0:128]
    planes[z, count : 2 * count] = power[:, 128:256]
    planes[z, 2 * count :] = jnp.concatenate([rest[:slab_rows], rest[slab_rows:]], axis=1)

    def deep_copy(i, slot):
        return pltpu.make_async_remote_copy(
            src_ref=planes.at[slot], dst_ref=planes.at[slot], send_sem=deep_send.at[i],
            recv_sem=deep_recv.at[slot], device_id=(((z + i) % deep) * near + flat, slab),
            device_id_type=MESH,
        )

    def near_copy(i, target, off, slot):
        return pltpu.make_async_remote_copy(
            src_ref=blocks.at[off * wide + i * 2 + target], dst_ref=landed.at[slot],
            send_sem=near_send, recv_sem=near_recv.at[here],
            device_id=(z * near + (flat + i) % near, target * 2 + core), device_id_type=MESH,
        )

    order = sorted(range(1, deep), key=lambda i: (min(i, deep - i), i))
    for i in order:
        deep_copy(i, z).start()
    lane = lax.broadcasted_iota(jnp.int32, (slab_rows, 128), 1)
    stages = [[0]] + [order[i : i + 2] for i in range(0, deep - 1, 2)]
    for stage in stages:
        lefts = []
        for off in stage:
            slot = (z + off) % deep
            if off > 0:
                deep_copy(off, slot).wait_recv()
            block = planes[slot]
            rest = block[2 * count :].astype(F32)
            rest = jnp.concatenate(
                [jnp.where(lane < 64, rest, 0.0), jnp.where(lane >= 64, rest, 0.0)], axis=0
            ).astype(BF16)
            lefts.append(
                jnp.concatenate([block[0:count], block[count : 2 * count], rest], axis=1)
            )
        left = lefts[0] if len(lefts) == 1 else jnp.concatenate(lefts, axis=0)
        got = jnp.dot(left, picks[...], preferred_element_type=F32).astype(BF16)
        for n, off in enumerate(stage):
            for i in range(near):
                for target in range(2):
                    at = n * count + target * slab_rows
                    blocks[off * wide + i * 2 + target] = got[
                        at : at + slab_rows, i * width : (i + 1) * width
                    ]
            slot = here * deep + (z + off) % deep
            near_copy(0, 1 - far, off, slot).start()

            @pl.loop(1, near)
            def _(i):
                near_copy(i, 0, off, slot).start()
                near_copy(i, 1, off, slot).start()

            landed[slot] = blocks[off * wide + far]

    for i in range(wide):
        source = (here + i) % wide
        at = pl.ds(source * deep, deep)
        if i > 0:
            pltpu.make_async_remote_copy(
                src_ref=landed.at[at], dst_ref=landed.at[at], send_sem=near_send,
                recv_sem=near_recv.at[source], device_id=pair, device_id_type=MESH,
            ).wait_recv()
        rows = deep * slab_rows
        wide_f[pl.ds(pl.multiple_of(source * rows, rows), rows), :] = (
            landed[at].astype(F32).reshape(rows, width)
        )
    for k in range(slab_rows):
        out_ref[:, k, :] = wide_f[pl.ds(k, wide * deep, stride=slab_rows), :].T
    for i in order:
        deep_copy(i, z).wait_send()
    for copy in spot_copies:
        copy.wait_send()
    swap.wait_send()
    gone = send.at[pl.ds(0, chips - 1)]
    pltpu.make_async_copy(gone, gone, send_sem).wait()
    gone = blocks.at[pl.ds(0, (wide - 1) * deep)]
    pltpu.make_async_copy(gone, gone, near_send).wait()


def on_device(smatrix, amplitude, beam_index, positions):
    _, beams_here, slab_rows, cols = smatrix.shape
    probes = lax.axis_size("probe")
    near = 8 if probes == 64 else 2
    deep = probes // near
    wide = 2 * near
    chips = 2 * probes
    slabs = lax.axis_size("slab")
    width = positions.shape[0]
    lanes = QUAD * slab_rows
    kdim = 4 * probes
    ctab = jnp.asarray(column_table(near, deep, cols))
    rtab = jnp.asarray(row_table(slab_rows, slabs))
    vmem = pl.BlockSpec(memory_space=pltpu.VMEM)
    hbm = pl.BlockSpec(memory_space=pltpu.HBM)
    dma = pltpu.SemaphoreType.DMA
    return pl.pallas_call(
        functools.partial(exchange, near, deep),
        out_shape=jax.ShapeDtypeStruct((width, slab_rows, cols), F32),
        in_specs=[vmem, vmem, vmem, vmem, hbm, hbm],
        out_specs=vmem,
        scratch_shapes=[
            pltpu.VMEM(ctab.shape, BF16),
            pltpu.VMEM(rtab.shape[1:], BF16),
            pltpu.VMEM((chips * 4, lanes), F32),
            pltpu.VMEM((chips, 4, lanes), BF16),
            pltpu.VMEM((chips, 4, lanes), BF16),
            pltpu.VMEM((chips, 4, lanes), BF16),
            pltpu.VMEM((2 * QUAD * SPOTS, kdim), BF16),
            pltpu.VMEM((SPOTS, 8 * lanes), BF16),
            pltpu.VMEM((SPOTS, 8 * lanes), BF16),
            pltpu.VMEM((deep, 5 * slab_rows, 128), BF16),
            pltpu.VMEM((384, near * width), BF16),
            pltpu.VMEM((8, width), F32),
            pltpu.VMEM((near, 8, width), F32),
            pltpu.VMEM((wide * deep, slab_rows, width), BF16),
            pltpu.VMEM((wide * deep, slab_rows, width), BF16),
            pltpu.VMEM((wide * deep * slab_rows, width), F32),
            dma, dma, dma, dma, dma, dma,
            dma((deep,)), dma((deep,)), dma((near,)), dma((near,)), dma, dma((wide,)),
        ],
        compiler_params=pltpu.CompilerParams(
            collective_id=0, has_side_effects=True, vmem_limit_bytes=48 * 1024 * 1024
        ),
    )(smatrix, amplitude, beam_index.T, positions.T, ctab, rtab)


def solution(mesh):
    return jax.shard_map(
        on_device,
        mesh=mesh,
        in_specs=(P(None, "probe", "slab", None), P(), P(), P("probe", None)),
        out_specs=P("probe", "slab", None),
        check_vma=False,
    )
```

time: 61.5 us -> 51.4 us (0.84)
  Pallas kernels: 56.5 us -> 44.6 us
  local copies, waits for them, and re-layouts: 2.87 us -> 6.45 us
  other arithmetic: 1.78 us -> 0 us
    pallas_call x2 -> x1, Pallas kernels: 56.5 us -> 44.6 us  [on_device(): pl.pallas_call(functools.partial(exchange, near, deep), out_shape=jax.Sha...]
    unnamed x8 -> x13, local copies, waits for them, and re-layouts: 0.99 us -> 6.45 us
    convert_element_type x2 -> x0, other arithmetic: 1.5 us -> none  [the longest x1 0.81 us: on_device(): ((positions[:, 0] + HALO) * SIDE + positions[:, 1] + HALO).astype(F32)]
    slice x2 -> x0, local copies, waits for them, and re-layouts: 0.81 us -> none  [the longest x1 0.78 us: on_device(): amplitude[1]]
where the time goes in v3:
time: 51.4 us; the launch traced here: 51.1 us
  Pallas kernels  44.6 us (87%)
  local copies, waits for them, and re-layouts  6.45 us (13%)
    pallas_call x1, Pallas kernels, on_device(): pl.pallas_call(functools.partial(exchange, near, deep), out_shape=jax.Sha...  44.6 us
    unnamed x13, local copies, waits for them, and re-layouts  6.45 us

profile of v3, /device:TPU:1, one launch (start us, length us, event | category | flops | bytes accessed | tf_op | source)
XLA Modules:
  0.0 51.1 jit_solution(3034651794646094768)
XLA Ops:
  0.0 0.0 copy-start
  0.0 1.2 %copy-done = bf16[2,2,128,1024]{3,2,1,0:T(8,128)(2,1)S(1)} copy-done((bf16[2,2,128,1024]{3,2,1,0:T(8,128)(2,1)S(1)}, bf16[2,2,128,1024]{3,2,1,0:T(8,128)(2,1)}, u32[]{:S(2)}) %copy-start) | copy-done | bytes 1048600
  1.2 0.0 copy-start.1
  1.2 0.9 %copy-done.1 = bf16[2,256,256]{2,1,0:T(8,128)(2,1)S(1)} copy-done((bf16[2,256,256]{2,1,0:T(8,128)(2,1)S(1)}, bf16[2,256,256]{2,1,0:T(8,128)(2,1)}, u32[]{:S(2)}) %copy-start.1) | copy-done | bytes 262168
  2.2 0.0 copy-start.2
  2.2 0.9 %copy-done.2 = bf16[2,8,32,128]{3,2,1,0:T(8,128)(2,1)S(1)} copy-done((bf16[2,8,32,128]{3,2,1,0:T(8,128)(2,1)S(1)}, bf16[2,8,32,128]{3,2,1,0:T(8,128)(2,1)}, u32[]{:S(2)}) %copy-start.2) | copy-done | bytes 131096
  3.1 0.0 copy-start.3
  3.1 0.7 %copy-done.3 = f32[2,512]{1,0:T(2,128)S(1)} copy-done((f32[2,512]{1,0:T(2,128)S(1)}, f32[2,512]{1,0:T(2,128)}, u32[]{:S(2)}) %copy-start.3) | copy-done | bytes 4120
  3.8 0.0 copy-start.4
  3.8 0.7 %copy-done.4 = s32[512,2]{0,1:T(2,128)S(1)} copy-done((s32[512,2]{0,1:T(2,128)S(1)}, s32[512,2]{0,1:T(2,128)}, u32[]{:S(2)}) %copy-start.4) | copy-done | bytes 4120
  4.5 0.0 copy-start.5
  4.5 0.7 %copy-done.5 = s32[128,2]{0,1:T(2,128)S(1)} copy-done((s32[128,2]{0,1:T(2,128)S(1)}, s32[128,2]{0,1:T(2,128)}, u32[]{:S(2)}) %copy-start.5) | copy-done | bytes 1048
  5.1 44.6 %shard_map.64 = f32[128,32,128]{2,1,0:T(8,128)S(1)} custom-call(bf16[2,8,32,128]{3,2,1,0:T(8,128)(2,1)S(1)} %copy-done.2, f32[2,512]{1,0:T(2,128)S(1)} %copy-done.3, s32[2,512]{1,0:T(2,128)S(1)} %bitcast.2, s32[2,128]{1,0:T(2,128)S(1)} %bitcast.3, bf16[2,256,256]{2,1,0:T(8,128)(2,1)S(1)} %copy-done.1, bf16[2,2,128,1024]{3,2,1,0:T(8,128)(2,1)S(1)} %copy-done), custom_call_target="tpu_custom_call" | custom-call | tf_op jit(solution)/shard_map/pallas_call | solution.py:335
  49.8 1.3 %copy.8 = f32[128,32,128]{2,1,0:T(8,128)} copy(f32[128,32,128]{2,1,0:T(8,128)S(1)} %shard_map.64) | data formatting | bytes 4194304
Async XLA Ops:
  0.0 1.2 %copy-start = (bf16[2,2,128,1024]{3,2,1,0:T(8,128)(2,1)S(1)}, bf16[2,2,128,1024]{3,2,1,0:T(8,128)(2,1)}, u32[]{:S(2)}) copy-start(bf16[2,2,128,1024]{3,2,1,0:T(8,128)(2,1)} %constant.5.clone.rtab_hbm) | copy-start | bytes 3145732
  1.2 0.9 %copy-start.1 = (bf16[2,256,256]{2,1,0:T(8,128)(2,1)S(1)}, bf16[2,256,256]{2,1,0:T(8,128)(2,1)}, u32[]{:S(2)}) copy-start(bf16[2,256,256]{2,1,0:T(8,128)(2,1)} %constant.4.clone.ctab_hbm) | copy-start | bytes 786436
  2.2 0.9 %copy-start.2 = (bf16[2,8,32,128]{3,2,1,0:T(8,128)(2,1)S(1)}, bf16[2,8,32,128]{3,2,1,0:T(8,128)(2,1)}, u32[]{:S(2)}) copy-start(bf16[2,8,32,128]{3,2,1,0:T(8,128)(2,1)} %s_ref.1) | copy-start | bytes 393220
  3.1 0.7 %copy-start.3 = (f32[2,512]{1,0:T(2,128)S(1)}, f32[2,512]{1,0:T(2,128)}, u32[]{:S(2)}) copy-start(f32[2,512]{1,0:T(2,128)} %amp_ref.1) | copy-start | bytes 12292
  3.8 0.7 %copy-start.4 = (s32[512,2]{0,1:T(2,128)S(1)}, s32[512,2]{0,1:T(2,128)}, u32[]{:S(2)}) copy-start(s32[512,2]{0,1:T(2,128)} %param.8) | copy-start | bytes 12292
  4.5 0.7 %copy-start.5 = (s32[128,2]{0,1:T(2,128)S(1)}, s32[128,2]{0,1:T(2,128)}, u32[]{:S(2)}) copy-start(s32[128,2]{0,1:T(2,128)} %param.9) | copy-start | bytes 3076

commit v4 on v3

--- a/solution.py
+++ b/solution.py
@@ -43,7 +43,7 @@
         )
         row = np.concatenate(
             [
-                np.tile((far * 2 + side) * slab_rows + np.arange(slab_rows), QUAD)
+                (far * 2 + side) * slab_rows + np.arange(slab_rows)
                 for side in (core, 1 - core)
                 for far in range(2)
             ]
@@ -103,10 +103,10 @@
 
 def exchange(
     near, deep,
-    s_ref, amp_ref, freq_ref, place_ref, ctab_hbm, rtab_hbm, out_ref,
-    ctab, rtab, sendf, send, field, other, weight, high, low, planes, picks, spot, spots,
+    s_hbm, amp_hbm, freq_hbm, place_hbm, ctab_hbm, rtab_hbm, out_ref,
+    s_ref, amp_ref, freq_ref, place_ref, ctab, rtab, sendf, send, field, other, beams_f, weight, planes, picks, spot, spots,
     blocks, landed, wide_f,
-    ctab_sem, rtab_sem, send_sem, recv_sem, pair_send, pair_recv,
+    s_sem, amp_sem, freq_sem, place_sem, ctab_sem, rtab_sem, send_sem, recv_sem, pair_send, pair_recv,
     deep_send, deep_recv, spot_send, spot_recv, near_send, near_recv,
 ):
     probe, slab = lax.axis_index("probe"), lax.axis_index("slab")
@@ -125,19 +125,34 @@
     pair = (probe, far * 2 + 1 - core)
     barrier = pltpu.get_barrier_semaphore()
 
-    @pl.loop(1, chips)
-    def _(i):
-        pl.semaphore_signal(barrier, inc=1, device_id=device((chip + i) % chips), device_id_type=MESH)
-
+    def others(body):
+        for dz in sorted(range(deep), key=lambda i: -min(i, deep - i)):
+
+            @pl.loop(0 if dz else 1, wide)
+            def _(e):
+                at = (here + e) % wide
+                body((at // near) * probes + ((z + dz) % deep) * near + at % near)
+
+    others(
+        lambda to: pl.semaphore_signal(
+            barrier, inc=1, device_id=device(to), device_id_type=MESH
+        )
+    )
     pl.semaphore_signal(barrier, inc=1, device_id=pair, device_id_type=MESH)
+    s_copy = pltpu.make_async_copy(s_hbm, s_ref, s_sem)
     ctab_copy = pltpu.make_async_copy(ctab_hbm, ctab, ctab_sem)
-    ctab_copy.start()
+    place_copy = pltpu.make_async_copy(place_hbm, place_ref, place_sem)
+    amp_copy = pltpu.make_async_copy(amp_hbm, amp_ref, amp_sem)
+    freq_copy = pltpu.make_async_copy(freq_hbm, freq_ref, freq_sem)
     rtab_copy = pltpu.make_async_copy(rtab_hbm.at[core], rtab, rtab_sem)
-    rtab_copy.start()
+    for copy in (s_copy, ctab_copy, place_copy, amp_copy, freq_copy, rtab_copy):
+        copy.start()
+    place_copy.wait()
     width = place_ref.shape[1]
     index = (place_ref[0:1, :] + HALO) * SIDE + place_ref[1:2, :] + HALO
     spot[...] = jnp.broadcast_to(index.astype(F32), (8, width))
 
+    s_copy.wait()
     ctab_copy.wait()
     parts = [s_ref[part].reshape(beams_here * slab_rows, cols) for part in range(2)]
     both = jnp.concatenate(parts, axis=1)
@@ -152,14 +167,12 @@
     spots[flat] = spot[...]
     pl.semaphore_wait(barrier, chips)
 
-    @pl.loop(1, chips)
-    def _(i):
-        to = (chip + i) % chips
-        pltpu.make_async_remote_copy(
+    others(
+        lambda to: pltpu.make_async_remote_copy(
             src_ref=send.at[to], dst_ref=field.at[chip], send_sem=send_sem, recv_sem=recv_sem,
             device_id=device(to), device_id_type=MESH,
         ).start()
-
+    )
     pltpu.make_async_copy(send.at[chip], field.at[chip], recv_sem).start()
     spot_copies = []
     for i in range(1, near):
@@ -171,50 +184,17 @@
         copy.start()
         spot_copies.append(copy)
 
-    kdim = weight.shape[1]
+    amp_copy.wait()
+    freq_copy.wait()
+    kdim = 4 * probes
     f0, f1, amp_re, amp_im = beam_rows(amp_ref, freq_ref, probes)
     r0, c0 = spot_offsets(kdim)
     for j in range(QUAD):
         at = slice(j * kdim, (j + 1) * kdim)
         cos, sin = unit_circle((f0[:, at] * r0 + f1[:, at] * c0) * (1.0 / (4 * slab_rows)))
         re, im = amp_re[:, at], amp_im[:, at]
-        weight[j * SPOTS : (j + 1) * SPOTS, :] = (re * cos + im * sin).astype(BF16)
-        weight[(4 + j) * SPOTS : (5 + j) * SPOTS, :] = (im * cos - re * sin).astype(BF16)
-
-    pltpu.make_async_copy(field, field, recv_sem).wait()
-    swap = pltpu.make_async_remote_copy(
-        src_ref=field, dst_ref=other, send_sem=pair_send, recv_sem=pair_recv,
-        device_id=pair, device_id_type=MESH,
-    )
-    swap.start()
-
-    def beam_sum(source, side, turn):
-        r0, _ = spot_offsets(2 * lanes)
-        lane = lax.broadcasted_iota(jnp.int32, (SPOTS, 2 * lanes), 1)
-        group = (lane % lanes) // slab_rows
-        row = ((lane // lanes) * 2 + side) * slab_rows + lane % slab_rows
-        rowf = row.astype(F32)
-        inside = (rowf >= r0) & (rowf < r0 + 4.0 * slab_rows)
-        x = jnp.concatenate(
-            [
-                source[0:probes].reshape(probes * 4, lanes),
-                source[probes : 2 * probes].reshape(probes * 4, lanes),
-            ],
-            axis=1,
-        )
-        for part in range(2):
-            total = None
-            for j in range(QUAD):
-                w = weight[(part * QUAD + j) * SPOTS : (part * QUAD + j + 1) * SPOTS, :]
-                y = jnp.dot(w, x, preferred_element_type=F32)
-                total = y if j == 0 else jnp.where(group == j, y, total)
-            total = jnp.where(inside, total, 0.0)
-            top = total.astype(BF16)
-            at = (part * 2 + turn) * 2 * lanes
-            high[:, at : at + 2 * lanes] = top
-            low[:, at : at + 2 * lanes] = (total - top.astype(F32)).astype(BF16)
-
-    beam_sum(field, core, 0)
+        weight[0:SPOTS, at] = (re * cos + im * sin).astype(BF16)
+        weight[SPOTS:, at] = (im * cos - re * sin).astype(BF16)
     for i in range(near):
         at = (flat + i) % near
         if i > 0:
@@ -226,10 +206,44 @@
         row = jnp.where(row >= 320, row - 64, row).astype(F32)
         hit = row == spots[at][0:1, :]
         picks[:, i * width : (i + 1) * width] = jnp.where(hit, 1.0, 0.0).astype(BF16)
+
+    pltpu.make_async_copy(field, field, recv_sem).wait()
+    swap = pltpu.make_async_remote_copy(
+        src_ref=field, dst_ref=other, send_sem=pair_send, recv_sem=pair_recv,
+        device_id=pair, device_id_type=MESH,
+    )
+    swap.start()
+
+    group = lax.broadcasted_iota(jnp.int32, (kdim, lanes), 1) // slab_rows
+
+    def spread(source, turn):
+        for far_of in range(2):
+            t = turn * 2 + far_of
+            x = source[far_of * probes : (far_of + 1) * probes].reshape(kdim, lanes).astype(F32)
+            for j in range(QUAD):
+                shift = ((t - j) % QUAD) * slab_rows
+                moved = pltpu.roll(x, shift, 1) if shift else x
+                at = slice(j * kdim, (j + 1) * kdim)
+                sofar = moved if t == 0 else jnp.where(group == t, moved, beams_f[at, :])
+                beams_f[at, :] = sofar
+
+    spread(field, 0)
     swap.wait_recv()
-    beam_sum(other, 1 - core, 1)
+    spread(other, 1)
+    total = jnp.dot(weight[...], beams_f[...].astype(BF16), preferred_element_type=F32)
+    r0, _ = spot_offsets(lanes)
+    lane = lax.broadcasted_iota(jnp.int32, (SPOTS, lanes), 1)
+    t = lane // slab_rows
+    side = jnp.where(t < 2, core, 1 - core)
+    row = (((t % 2) * 2 + side) * slab_rows + lane % slab_rows).astype(F32)
+    inside = (row >= r0) & (row < r0 + 4.0 * slab_rows)
+    both = jnp.concatenate(
+        [jnp.where(inside, total[0:SPOTS], 0.0), jnp.where(inside, total[SPOTS:], 0.0)], axis=1
+    )
+    high = both.astype(BF16)
+    low = (both - high.astype(F32)).astype(BF16)
     rtab_copy.wait()
-    out = nt(rtab[0], high[...]) + (nt(rtab[0], low[...]) + nt(rtab[1], high[...]))
+    out = nt(rtab[0], high) + (nt(rtab[0], low) + nt(rtab[1], high))
     count = 2 * slab_rows
     re, im = out[:count], out[count:]
     scale = 1.0 / (4 * slab_rows * chips)
@@ -239,11 +253,11 @@
     planes[z, count : 2 * count] = power[:, 128:256]
     planes[z, 2 * count :] = jnp.concatenate([rest[:slab_rows], rest[slab_rows:]], axis=1)
 
-    def deep_copy(i, slot):
+    def deep_copy(i, slot, send_at, recv_at, rows=slice(None)):
         return pltpu.make_async_remote_copy(
-            src_ref=planes.at[slot], dst_ref=planes.at[slot], send_sem=deep_send.at[i],
-            recv_sem=deep_recv.at[slot], device_id=(((z + i) % deep) * near + flat, slab),
-            device_id_type=MESH,
+            src_ref=planes.at[slot, rows], dst_ref=planes.at[slot, rows],
+            send_sem=deep_send.at[send_at], recv_sem=deep_recv.at[recv_at],
+            device_id=(((z + i) % deep) * near + flat, slab), device_id_type=MESH,
         )
 
     def near_copy(i, target, off, slot):
@@ -253,18 +267,12 @@
             device_id=(z * near + (flat + i) % near, target * 2 + core), device_id_type=MESH,
         )
 
-    order = sorted(range(1, deep), key=lambda i: (min(i, deep - i), i))
-    for i in order:
-        deep_copy(i, z).start()
     lane = lax.broadcasted_iota(jnp.int32, (slab_rows, 128), 1)
-    stages = [[0]] + [order[i : i + 2] for i in range(0, deep - 1, 2)]
-    for stage in stages:
+
+    def pick_and_send(stage):
         lefts = []
         for off in stage:
-            slot = (z + off) % deep
-            if off > 0:
-                deep_copy(off, slot).wait_recv()
-            block = planes[slot]
+            block = planes[(z + off) % deep]
             rest = block[2 * count :].astype(F32)
             rest = jnp.concatenate(
                 [jnp.where(lane < 64, rest, 0.0), jnp.where(lane >= 64, rest, 0.0)], axis=0
@@ -291,6 +299,47 @@
 
             landed[slot] = blocks[off * wide + far]
 
+    def arrived(off, recv_at=None, rows=slice(None)):
+        slot = (z + off) % deep
+        deep_copy(off, slot, 0, slot if recv_at is None else recv_at, rows).wait_recv()
+
+    sent = []
+
+    def pass_on(i, off, recv_at=None, rows=slice(None)):
+        slot = (z + off) % deep
+        copy = deep_copy(i, slot, len(sent), slot if recv_at is None else recv_at, rows)
+        copy.start()
+        sent.append(copy)
+
+    if deep == 8:
+        first, second = slice(0, 80), slice(80, 160)
+        for i in (1, 7, 2, 6):
+            pass_on(i, 0)
+        pick_and_send([0])
+        arrived(1)
+        arrived(7)
+        pick_and_send([1, 7])
+        arrived(2)
+        arrived(6)
+        pass_on(7, 2)
+        pass_on(1, 6)
+        pass_on(2, 6, None, first)
+        pass_on(6, 2, deep, second)
+        pick_and_send([2, 6])
+        arrived(3)
+        arrived(5)
+        pick_and_send([3, 5])
+        arrived(4, None, first)
+        arrived(4, deep, second)
+        pick_and_send([4])
+    else:
+        for i in range(1, deep):
+            pass_on(i, 0)
+        pick_and_send([0])
+        for i in range(1, deep):
+            arrived(i)
+            pick_and_send([i])
+
     for i in range(wide):
         source = (here + i) % wide
         at = pl.ds(source * deep, deep)
@@ -305,9 +354,7 @@
         )
     for k in range(slab_rows):
         out_ref[:, k, :] = wide_f[pl.ds(k, wide * deep, stride=slab_rows), :].T
-    for i in order:
-        deep_copy(i, z).wait_send()
-    for copy in spot_copies:
+    for copy in sent + spot_copies:
         copy.wait_send()
     swap.wait_send()
     gone = send.at[pl.ds(0, chips - 1)]
@@ -319,7 +366,7 @@
 def on_device(smatrix, amplitude, beam_index, positions):
     _, beams_here, slab_rows, cols = smatrix.shape
     probes = lax.axis_size("probe")
-    near = 8 if probes == 64 else 2
+    near = max(1, probes // 8)
     deep = probes // near
     wide = 2 * near
     chips = 2 * probes
@@ -329,24 +376,28 @@
     kdim = 4 * probes
     ctab = jnp.asarray(column_table(near, deep, cols))
     rtab = jnp.asarray(row_table(slab_rows, slabs))
+    operands = (smatrix, amplitude, beam_index.T, positions.T, ctab, rtab)
     vmem = pl.BlockSpec(memory_space=pltpu.VMEM)
     hbm = pl.BlockSpec(memory_space=pltpu.HBM)
     dma = pltpu.SemaphoreType.DMA
     return pl.pallas_call(
         functools.partial(exchange, near, deep),
         out_shape=jax.ShapeDtypeStruct((width, slab_rows, cols), F32),
-        in_specs=[vmem, vmem, vmem, vmem, hbm, hbm],
+        in_specs=[hbm] * 6,
         out_specs=vmem,
         scratch_shapes=[
+            pltpu.VMEM(smatrix.shape, BF16),
+            pltpu.VMEM(amplitude.shape, F32),
+            pltpu.VMEM((2, amplitude.shape[1]), jnp.int32),
+            pltpu.VMEM((2, width), jnp.int32),
             pltpu.VMEM(ctab.shape, BF16),
             pltpu.VMEM(rtab.shape[1:], BF16),
             pltpu.VMEM((chips * 4, lanes), F32),
             pltpu.VMEM((chips, 4, lanes), BF16),
             pltpu.VMEM((chips, 4, lanes), BF16),
             pltpu.VMEM((chips, 4, lanes), BF16),
-            pltpu.VMEM((2 * QUAD * SPOTS, kdim), BF16),
-            pltpu.VMEM((SPOTS, 8 * lanes), BF16),
-            pltpu.VMEM((SPOTS, 8 * lanes), BF16),
+            pltpu.VMEM((QUAD * kdim, lanes), F32),
+            pltpu.VMEM((2 * SPOTS, QUAD * kdim), BF16),
             pltpu.VMEM((deep, 5 * slab_rows, 128), BF16),
             pltpu.VMEM((384, near * width), BF16),
             pltpu.VMEM((8, width), F32),
@@ -354,13 +405,13 @@
             pltpu.VMEM((wide * deep, slab_rows, width), BF16),
             pltpu.VMEM((wide * deep, slab_rows, width), BF16),
             pltpu.VMEM((wide * deep * slab_rows, width), F32),
-            dma, dma, dma, dma, dma, dma,
-            dma((deep,)), dma((deep,)), dma((near,)), dma((near,)), dma, dma((wide,)),
+            dma, dma, dma, dma, dma, dma, dma, dma, dma, dma,
+            dma((deep,)), dma((deep + 1,)), dma((near,)), dma((near,)), dma, dma((wide,)),
         ],
         compiler_params=pltpu.CompilerParams(
             collective_id=0, has_side_effects=True, vmem_limit_bytes=48 * 1024 * 1024
         ),
-    )(smatrix, amplitude, beam_index.T, positions.T, ctab, rtab)
+    )(*[pltpu.with_memory_space_constraint(v, pltpu.HBM) for v in operands])
 
 
 def solution(mesh):

time: 51.4 us -> 46.6 us (0.907)
  local copies, waits for them, and re-layouts: 6.45 us -> 1.32 us
  Pallas kernels: 44.6 us -> 45.2 us
    unnamed x13 -> x1, local copies, waits for them, and re-layouts: 6.45 us -> 1.32 us
where the time goes in v4:
time: 46.6 us; the launch traced here: 46.5 us
  Pallas kernels  45.2 us (97%)
  local copies, waits for them, and re-layouts  1.32 us (3%)
    pallas_call x1, Pallas kernels, on_device(): pl.pallas_call(functools.partial(exchange, near, deep), out_shape=jax.Sha...  45.2 us
    unnamed x1, local copies, waits for them, and re-layouts  1.32 us

profile of v4, /device:TPU:1, one launch (start us, length us, event | category | flops | bytes accessed | tf_op | source)
XLA Modules:
  0.0 46.5 jit_solution(1849497792888806118)
XLA Ops:
  0.0 45.2 %shard_map.64 = f32[128,32,128]{2,1,0:T(8,128)S(1)} custom-call(bf16[2,8,32,128]{3,2,1,0:T(8,128)(2,1)} %s_hbm.1, f32[2,512]{1,0:T(2,128)} %amp_hbm.1, s32[2,512]{1,0:T(2,128)} %bitcast.2, s32[2,128]{1,0:T(2,128)} %bitcast.3, bf16[2,256,256]{2,1,0:T(8,128)(2,1)} %constant.4.clone.ctab_hbm, bf16[2,2,128,256]{3,2,1,0:T(8,128)(2,1)} %constant.5.clone.rtab_hbm), custom_call_target="tpu_custom_call" | custom-call | tf_op jit(solution)/shard_map/pallas_call | solution.py:383
  45.2 1.3 %copy.8 = f32[128,32,128]{2,1,0:T(8,128)} copy(f32[128,32,128]{2,1,0:T(8,128)S(1)} %shard_map.64) | data formatting | bytes 4194304
